TPU v7x, 512 devices: a whole 4x4x16 slice. The times are simulated.
512 devices in a mesh: sec: 32 (over z, core), term: 16 (over y, x).
Axes of the slice: x: 4, y: 4, z: 16, core: 2. Of those that a mesh axis runs over, the one named last changes fastest.
Arguments:
- psi: bfloat16 [128, 4, 256, 256], P('sec'), may hold values from -6 to 6
- left_env: bfloat16 [64, 128, 256, 256], P('term', 'sec'), may hold values from -0.046875 to 0.046875
- right_env: bfloat16 [64, 256, 256], P('term'), may hold values from -0.375 to 0.375
- site_ops: float32 [64, 4, 4], P('term'), may hold values from -3 to 3
- coupling: int32 [64, 128], P('term', 'sec'), may hold values from -1 to 127, as said below
- live: int32 [128], P('sec'), may hold values from 128 to 256, as said below
Outputs:
- sigma: bfloat16 [128, 4, 256, 256], P('sec', None, 'term')
Inputs may be any that keep to these rules, and one draw needn't show every extreme that they name: coupling[t, s] is -1 or a block within 2 of s; some terms couple at distance 2 in both directions. live sizes are at least 128.
All inputs are finite; a program needn't handle non-finite values.
Results may differ from a plain program's by a relative error of at most 0.018.
Values may be sent and summed in bfloat16 or wider, within the bound.
A program may use at most 64 MiB of HBM per device.

v0:
```python
import jax
import jax.numpy as jnp
from jax import lax
from jax.sharding import PartitionSpec as P


def with_halo(value, sides, width):
    for axis, dim in sides:
        devices, length = (lax.axis_size(axis), value.shape[dim])
        up = [(i, (i + 1) % devices) for i in range(devices - 1)]
        down = [(j, i) for i, j in up]
        last = lax.slice_in_dim(value, length - width, length, axis=dim)
        first = lax.slice_in_dim(value, 0, width, axis=dim)
        before = lax.ppermute(last, axis, up)
        after = lax.ppermute(first, axis, down)
        value = jnp.concatenate([before, value, after], axis=dim)
    return value


def on_device(psi, left_env, right_env, site_ops, coupling, live):
    sec_count = psi.shape[0]
    width = psi.shape[2]
    row_count = width // lax.axis_size("term")
    row_start = lax.axis_index("term") * row_count
    extended = with_halo(psi, (("sec", 0),), 2)
    sec_base = lax.axis_index("sec") * sec_count

    def term_step(acc, inputs):
        left_t, right_t, ops_t, couple_t = inputs
        valid = couple_t >= 0
        index = jnp.where(valid, couple_t - sec_base + 2, 0)
        source = extended[index]
        mixed = jnp.einsum("kj,sjab->skab", ops_t, source.astype(jnp.float32))
        mixed = (mixed * valid[:, None, None, None].astype(jnp.float32)).astype(jnp.bfloat16)
        inner = jnp.einsum(
            "sab,skbc->skac", left_t, mixed, preferred_element_type=jnp.float32
        ).astype(jnp.bfloat16)
        outer = jnp.einsum("skac,cd->skad", inner, right_t, preferred_element_type=jnp.float32)
        return (acc + outer, None)

    start = jnp.zeros(psi.shape, jnp.float32)
    total, unused = lax.scan(term_step, start, (left_env, right_env, site_ops, coupling))
    mine = lax.psum_scatter(total, "term", scatter_dimension=2, tiled=True)
    rows_here = row_start + jnp.arange(row_count, dtype=jnp.int32)
    columns = jnp.arange(width, dtype=jnp.int32)
    rows_ok = rows_here[None, :] < live[:, None]
    cols_ok = columns[None, :] < live[:, None]
    keep = rows_ok[:, :, None] & cols_ok[:, None, :]
    result = jnp.where(keep[:, None, :, :], mine, 0.0)
    return result.astype(jnp.bfloat16)


def solution(mesh):
    placed = (
        P("sec", None, None, None),
        P("term", "sec", None, None),
        P("term", None, None),
        P("term", None, None),
        P("term", "sec"),
        P("sec"),
    )
    return jax.shard_map(
        on_device,
        mesh=mesh,
        in_specs=placed,
        out_specs=P("sec", None, "term", None),
        check_vma=False,
    )
```

profile of v0, /device:TPU:2, one launch (start us, length us, event | category | flops | bytes accessed | tf_op | source)
XLA Modules:
  0.0 192.1 jit_solution(12051327301831226384)
XLA Ops:
  6.5 2.8 %fusion.27 = (bf16[2,4,256,256]{3,2,1,0:T(8,128)(2,1)}, bf16[2,4,256,256]{3,2,1,0:T(8,128)(2,1)S(1)}) fusion(bf16[4,4,256,256]{3,2,1,0:T(8,128)(2,1)} %param.8), kind=kLoop, calls=%fused_computation.33 | loop fusion | bytes 4194304 | tf_op jit(solution)/shard_map/slice | solution.py:12
  9.4 2.7 %collective-permute-start = (bf16[2,4,256,256]{3,2,1,0:T(8,128)(2,1)}, bf16[2,4,256,256]{3,2,1,0:T(8,128)(2,1)}, u32[]{:S(2)}, u32[]{:S(2)}) collective-permute-start(bf16[2,4,256,256]{3,2,1,0:T(8,128)(2,1)} %get-tuple-element.91), channel_id=1, source_target_pairs={{0,16},{16,32},{32,48},{48,64},{64,80},{80,96},{96,112},{112,128},... | collective-permute-start | bytes 3145736 | tf_op jit(solution)/shard_map/ppermute | solution.py:14
  12.1 1.3 collective-permute-start.1
  13.4 0.3 collective-permute-done
  13.7 3.8 %collective-permute-done.1 = bf16[2,4,256,256]{3,2,1,0:T(8,128)(2,1)} collective-permute-done((bf16[2,4,256,256]{3,2,1,0:T(8,128)(2,1)S(1)}, bf16[2,4,256,256]{3,2,1,0:T(8,128)(2,1)}, u32[]{:S(2)}, u32[]{:S(2)}) %collective-permute-start.1) | collective-permute-done | bytes 1048608 | tf_op jit(solution)/shard_map/ppermute | solution.py:15
  17.5 3.4 %pad_maximum_fusion = bf16[8,4,256,256]{3,2,1,0:T(8,128)(2,1)} fusion(bf16[2,4,256,256]{3,2,1,0:T(8,128)(2,1)} %collective-permute-done.1, bf16[4,4,256,256]{3,2,1,0:T(8,128)(2,1)S(1)} %copy-done, bf16[2,4,256,256]{3,2,1,0:T(8,128)(2,1)} %collective-permute-done), kind=kLoop, calls=%fused_computation.27 | loop fusion | flops 4194304 | bytes 8388608 | tf_op jit(solution)/shard_map/concatenate | solution.py:16
  20.9 54.0 %while.11 = (s32[]{:T(128)}, f32[4,4,256,256]{3,2,1,0:T(8,128)}, s32[4,4]{1,0:T(4,128)S(1)}, s32[]{:T(128)}, bf16[8,4,256,256]{3,2,1,0:T(8,128)(2,1)}, /*index=5...) while((s32[]{:T(128)}, f32[4,4,256,256]{3,2,1,0:T(8,128)}, ...), condition=%wide.region_1.2_spmd.clone, body=%wide.region_0.1_spmd.clone.sunk | while | flops 1087374336 | bytes 23730416 | solution.py:42
  20.9 2.9 %gather_fusion = bf16[4,4,256,256]{3,2,1,0:T(8,128)(2,1)S(1)} fusion(bf16[8,4,256,256]{3,2,1,0:T(8,128)(2,1)} %get-tuple-element.166, s32[1024]{0:T(1024)S(1)} %pad_clamp_fusion.2), kind=kCustom, calls=%fused_computation.clone.clone.1 | custom fusion | bytes 4194320 | tf_op jit(solution)/shard_map/while/body/eval_jaxpr/gather | solution.py:32
  23.8 3.7 %fusion.44 = f32[4,256,256,4]{2,3,1,0:T(4,128)} fusion(bf16[4,4,256,256]{3,2,1,0:T(8,128)(2,1)S(1)} %gather_fusion, bf16[4,4,4]{2,1,0:T(4,128)(2,1)S(1)} %get-tuple-element.167, s32[]{:T(128)} %get-tuple-element.152), kind=kOutput, calls=%fused_computation.7.clone.1 | convolution fusion | flops 8388608 | bytes 6292484 | tf_op jit(solution)/shard_map/while/body/eval_jaxpr/kj,sjab->skab/dot_general | solution.py:33
  27.5 5.9 %select_add_fusion.2 = f32[4,4,256,256]{3,2,1,0:T(8,128)} fusion(f32[4,4,256,256]{3,2,1,0:T(8,128)} %get-tuple-element.153, pred[]{:T(512)S(6)} %compare.3, f32[4,256,256,4]{2,3,1,0:T(4,128)} %fusion.44, f32[4]{0:T(128)S(1)} %fusion.45, bf16[4,4,256,256]{3,2,1,0:T(8,128)(2,1)} %get-tuple-element.168, s32[]{:T(128)} %get-tuple-element.152, ...), kind=kOutput, calls=%fused_computation.3.clone.1 | convolution fusion | flops 1078984704 | bytes 13239313 | tf_op jit(solution)/shard_map/while/body/eval_jaxpr/skac,cd->skad/dot_general | solution.py:38
  33.4 2.9 %gather_fusion = bf16[4,4,256,256]{3,2,1,0:T(8,128)(2,1)S(1)} fusion(bf16[8,4,256,256]{3,2,1,0:T(8,128)(2,1)} %get-tuple-element.166, s32[1024]{0:T(1024)S(1)} %pad_clamp_fusion.2), kind=kCustom, calls=%fused_computation.clone.clone.1 | custom fusion | bytes 4194320 | tf_op jit(solution)/shard_map/while/body/eval_jaxpr/gather | solution.py:32
  36.3 3.7 %fusion.44 = f32[4,256,256,4]{2,3,1,0:T(4,128)} fusion(bf16[4,4,256,256]{3,2,1,0:T(8,128)(2,1)S(1)} %gather_fusion, bf16[4,4,4]{2,1,0:T(4,128)(2,1)S(1)} %get-tuple-element.167, s32[]{:T(128)} %get-tuple-element.152), kind=kOutput, calls=%fused_computation.7.clone.1 | convolution fusion | flops 8388608 | bytes 6292484 | tf_op jit(solution)/shard_map/while/body/eval_jaxpr/kj,sjab->skab/dot_general | solution.py:33
  40.0 7.2 %select_add_fusion.2 = f32[4,4,256,256]{3,2,1,0:T(8,128)} fusion(f32[4,4,256,256]{3,2,1,0:T(8,128)} %get-tuple-element.153, pred[]{:T(512)S(6)} %compare.3, f32[4,256,256,4]{2,3,1,0:T(4,128)} %fusion.44, f32[4]{0:T(128)S(1)} %fusion.45, bf16[4,4,256,256]{3,2,1,0:T(8,128)(2,1)} %get-tuple-element.168, s32[]{:T(128)} %get-tuple-element.152, ...), kind=kOutput, calls=%fused_computation.3.clone.1 | convolution fusion | flops 1078984704 | bytes 13239313 | tf_op jit(solution)/shard_map/while/body/eval_jaxpr/skac,cd->skad/dot_general | solution.py:38
  47.2 2.9 %gather_fusion = bf16[4,4,256,256]{3,2,1,0:T(8,128)(2,1)S(1)} fusion(bf16[8,4,256,256]{3,2,1,0:T(8,128)(2,1)} %get-tuple-element.166, s32[1024]{0:T(1024)S(1)} %pad_clamp_fusion.2), kind=kCustom, calls=%fused_computation.clone.clone.1 | custom fusion | bytes 4194320 | tf_op jit(solution)/shard_map/while/body/eval_jaxpr/gather | solution.py:32
  50.1 3.7 %fusion.44 = f32[4,256,256,4]{2,3,1,0:T(4,128)} fusion(bf16[4,4,256,256]{3,2,1,0:T(8,128)(2,1)S(1)} %gather_fusion, bf16[4,4,4]{2,1,0:T(4,128)(2,1)S(1)} %get-tuple-element.167, s32[]{:T(128)} %get-tuple-element.152), kind=kOutput, calls=%fused_computation.7.clone.1 | convolution fusion | flops 8388608 | bytes 6292484 | tf_op jit(solution)/shard_map/while/body/eval_jaxpr/kj,sjab->skab/dot_general | solution.py:33
  53.8 7.3 %select_add_fusion.2 = f32[4,4,256,256]{3,2,1,0:T(8,128)} fusion(f32[4,4,256,256]{3,2,1,0:T(8,128)} %get-tuple-element.153, pred[]{:T(512)S(6)} %compare.3, f32[4,256,256,4]{2,3,1,0:T(4,128)} %fusion.44, f32[4]{0:T(128)S(1)} %fusion.45, bf16[4,4,256,256]{3,2,1,0:T(8,128)(2,1)} %get-tuple-element.168, s32[]{:T(128)} %get-tuple-element.152, ...), kind=kOutput, calls=%fused_computation.3.clone.1 | convolution fusion | flops 1078984704 | bytes 13239313 | tf_op jit(solution)/shard_map/while/body/eval_jaxpr/skac,cd->skad/dot_general | solution.py:38
  61.1 2.9 %gather_fusion = bf16[4,4,256,256]{3,2,1,0:T(8,128)(2,1)S(1)} fusion(bf16[8,4,256,256]{3,2,1,0:T(8,128)(2,1)} %get-tuple-element.166, s32[1024]{0:T(1024)S(1)} %pad_clamp_fusion.2), kind=kCustom, calls=%fused_computation.clone.clone.1 | custom fusion | bytes 4194320 | tf_op jit(solution)/shard_map/while/body/eval_jaxpr/gather | solution.py:32
  64.0 3.7 %fusion.44 = f32[4,256,256,4]{2,3,1,0:T(4,128)} fusion(bf16[4,4,256,256]{3,2,1,0:T(8,128)(2,1)S(1)} %gather_fusion, bf16[4,4,4]{2,1,0:T(4,128)(2,1)S(1)} %get-tuple-element.167, s32[]{:T(128)} %get-tuple-element.152), kind=kOutput, calls=%fused_computation.7.clone.1 | convolution fusion | flops 8388608 | bytes 6292484 | tf_op jit(solution)/shard_map/while/body/eval_jaxpr/kj,sjab->skab/dot_general | solution.py:33
  67.6 7.2 %select_add_fusion.2 = f32[4,4,256,256]{3,2,1,0:T(8,128)} fusion(f32[4,4,256,256]{3,2,1,0:T(8,128)} %get-tuple-element.153, pred[]{:T(512)S(6)} %compare.3, f32[4,256,256,4]{2,3,1,0:T(4,128)} %fusion.44, f32[4]{0:T(128)S(1)} %fusion.45, bf16[4,4,256,256]{3,2,1,0:T(8,128)(2,1)} %get-tuple-element.168, s32[]{:T(128)} %get-tuple-element.152, ...), kind=kOutput, calls=%fused_computation.3.clone.1 | convolution fusion | flops 1078984704 | bytes 13239313 | tf_op jit(solution)/shard_map/while/body/eval_jaxpr/skac,cd->skad/dot_general | solution.py:38
  74.9 0.6 copy-done.3
  75.5 0.1 iota_compare_fusion
  75.7 0.1 broadcast_and_fusion
  75.8 107.9 %reduce-scatter.2.cloned.1.call-done = f32[4,4,16,256]{3,2,1,0:T(8,128)} async-done(((f32[4,4,256,256]{3,2,1,0:T(8,128)}), f32[4,4,16,256]{3,2,1,0:T(8,128)}) %reduce-scatter.2.cloned.1.call-update) | async-done | bytes 262160 | tf_op jit(solution)/shard_map/reduce_scatter | solution.py:43
  183.6 1.6 select_convert_fusion
  (25 shorter events, 0.2 us)
Async XLA Ops:
  6.5 11.0 %copy-start = (bf16[4,4,256,256]{3,2,1,0:T(8,128)(2,1)S(1)}, bf16[4,4,256,256]{3,2,1,0:T(8,128)(2,1)}, u32[]{:S(2)}) copy-start(bf16[4,4,256,256]{3,2,1,0:T(8,128)(2,1)} %param.8) | copy-start | bytes 6291460
  6.5 6.8 %copy-start.1 = (f32[4,4,4]{2,1,0:T(4,128)S(1)}, f32[4,4,4]{2,1,0:T(4,128)}, u32[]{:S(2)}) copy-start(f32[4,4,4]{2,1,0:T(4,128)} %param.11) | copy-start | bytes 772
  6.5 177.1 %reduce-scatter.2.cloned.1.call-start = ((), (), s32[]{:S(2)}) async-start(), calls=%async_computation.1 | async-start | bytes 4456448 | tf_op jit(solution)/shard_map/reduce_scatter | solution.py:43
  9.4 4.3 %collective-permute-start = (bf16[2,4,256,256]{3,2,1,0:T(8,128)(2,1)}, bf16[2,4,256,256]{3,2,1,0:T(8,128)(2,1)}, u32[]{:S(2)}, u32[]{:S(2)}) collective-permute-start(bf16[2,4,256,256]{3,2,1,0:T(8,128)(2,1)} %get-tuple-element.91), channel_id=1, source_target_pairs={{0,16},{16,32},{32,48},{48,64},{64,80},{80,96},{96,112},{112,128},... | collective-permute-start | bytes 3145736 | tf_op jit(solution)/shard_map/ppermute | solution.py:14
  12.1 5.4 %collective-permute-start.1 = (bf16[2,4,256,256]{3,2,1,0:T(8,128)(2,1)S(1)}, bf16[2,4,256,256]{3,2,1,0:T(8,128)(2,1)}, u32[]{:S(2)}, u32[]{:S(2)}) collective-permute-start(bf16[2,4,256,256]{3,2,1,0:T(8,128)(2,1)S(1)} %get-tuple-element.92), channel_id=1, source_target_pairs={{16,0},{32,16},{48,32},{64,48},{80,64},{96,80},{112,96},{128,112},... | collective-permute-start | bytes 3145736 | tf_op jit(solution)/shard_map/ppermute | solution.py:15
  13.4 7.5 %copy-start.2 = (s32[4,4]{1,0:T(4,128)S(1)}, s32[4,4]{1,0:T(4,128)}, u32[]{:S(2)}) copy-start(s32[4,4]{1,0:T(4,128)} %param.12) | copy-start | bytes 196
  74.9 0.7 copy-start.3
Sparse Core Ops, SparseCore 0:
  75.0 108.5 reduce-scatter.1
where the time goes:
time: 192 us
  waiting for transfers between devices  112 us (58%)
  matrix products  42.4 us (22%)
  local copies, waits for them, and re-layouts  14.9 us (8%)
  between operations  13.5 us (7%)
  other arithmetic  5.34 us (3%)
  starting transfers between devices  3.97 us (2%)
    reduce_scatter x1, waiting for transfers between devices, on_device(): mine = lax.psum_scatter(total, 'term', scatter_dimension=2, tiled=True)  108 us
    dot_general x4, matrix products, term_step(): jnp.einsum('skac,cd->skad', inner, right_t, preferred_element_type=jnp.fl...  27.7 us
    dot_general x4, matrix products, term_step(): mixed = jnp.einsum('kj,sjab->skab', ops_t, source.astype(jnp.float32))  14.7 us
    gather x4, local copies, waits for them, and re-layouts, term_step(): source = extended[index]  11.5 us
  transfers between devices with their start and end apart: 3, of which 3 were waited for; matrix products, arithmetic and copies ran while one was open for 0% of the time, Pallas kernels for 0%

commit v1 on v0

v1 whole, which is shorter than its diff:
```python
import functools

import jax
import jax.numpy as jnp
from jax import lax
from jax.experimental import pallas as pl
from jax.experimental.pallas import tpu as pltpu
from jax.sharding import PartitionSpec as P

MESH = pl.DeviceIdType.MESH
SIDE = 4
GROUPS = ((1, 2), (0, 3))


def kernel(
    sections, chunk,
    psi, left, right, ops, coupling, out,
    mid, far, lcat, rbuf, ybuf, acc, relay1, direct1, comb1, red, relay2, direct2, comb2,
    local_sem, halo_send, halo_recv, send1, recv1, send2, recv2,
):
    sec = lax.axis_index("sec")
    term = lax.axis_index("term")
    x, y = term % SIDE, term // SIDE
    up, down = (sec + 1) % sections, (sec + sections - 1) % sections
    near = (
        (y * SIDE + (x + 1) % SIDE, y * SIDE + (x + SIDE - 1) % SIDE),
        ((y + 1) % SIDE * SIDE + x, (y + SIDE - 1) % SIDE * SIDE + x),
    )
    place = (x, y)

    local = []

    def fetch(src, dst):
        copy = pltpu.make_async_copy(src, dst, local_sem.at[len(local)])
        copy.start()
        local.append(copy)

    fetch(psi, mid.at[pl.ds(1, 4)])
    fetch(right, rbuf)
    for t in range(4):
        for s in range(4):
            fetch(left.at[t, s], lcat.at[s, :, pl.ds(256 * t, 256)])

    barrier = pltpu.get_barrier_semaphore()
    for other in (up, down):
        pl.semaphore_signal(barrier, inc=1, device_id={"sec": other, "term": term}, device_id_type=MESH)
    for pair in near:
        for other in pair:
            pl.semaphore_signal(barrier, inc=1, device_id={"sec": sec, "term": other}, device_id_type=MESH)
    pl.semaphore_wait(barrier, 6)

    def halo(n, src, dst, other):
        copy = pltpu.make_async_remote_copy(
            src_ref=src, dst_ref=dst, send_sem=halo_send.at[n], recv_sem=halo_recv.at[n],
            device_id={"sec": other, "term": term}, device_id_type=MESH,
        )
        copy.start()
        return copy

    halos = [
        halo(0, psi.at[3], mid.at[0], up),
        halo(1, psi.at[0], mid.at[5], down),
        halo(2, psi.at[2], far.at[0], up),
        halo(3, psi.at[1], far.at[1], down),
    ]

    def compute(g, i, s):
        def term_step(t, carry):
            target = coupling[t, s]
            valid = target >= 0
            place_in = target - sec * 4
            index = jnp.clip(place_in + 1, 0, 5)
            is_far = jnp.logical_or(place_in == -2, place_in == 5)
            coef = [[jnp.where(valid, ops[t, k, j], 0.0) for j in range(4)] for k in range(4)]
            weights = rbuf[t]
            for r in range(0, 256, chunk):
                rows = pl.ds(r, chunk)
                source = []
                for j in range(4):
                    value = mid[index, j, rows, :]
                    if g == 1:
                        value = jnp.where(is_far, far[i, j, rows, :], value)
                    source.append(value.astype(jnp.float32))
                mixed = []
                for k in range(4):
                    total = coef[k][0] * source[0]
                    for j in range(1, 4):
                        total = total + coef[k][j] * source[j]
                    mixed.append(total.astype(jnp.bfloat16))
                inner = jnp.dot(
                    jnp.concatenate(mixed, axis=0), weights, preferred_element_type=jnp.float32
                ).astype(jnp.bfloat16)
                for k in range(4):
                    ybuf[t, rows, pl.ds(256 * k, 256)] = inner[k * chunk : (k + 1) * chunk]
            return carry

        lax.fori_loop(0, 4, term_step, 0)

        lhs = lcat[s]
        for k in range(4):
            rhs = ybuf[:, :, pl.ds(256 * k, 256)].reshape(1024, 256)
            total = jnp.dot(lhs, rhs, preferred_element_type=jnp.float32)
            acc[g, i, k] = total.astype(jnp.bfloat16).reshape(SIDE, SIDE, 16, 256)

    pending = []

    def send(src, dst, send_sem, recv_sem, axis, direction):
        copy = pltpu.make_async_remote_copy(
            src_ref=src, dst_ref=dst, send_sem=send_sem, recv_sem=recv_sem,
            device_id={"sec": sec, "term": near[axis][direction]}, device_id_type=MESH,
        )
        copy.start()
        pending.append(copy)
        return copy

    def slab(g, h, d, at):
        if h == 0:
            return (g, slice(None), d, slice(None), at)
        return (g, slice(None), 2 + d, at)

    copies = {}

    def first(g, h):
        at = place[h]
        opposite = (at + 2) % SIDE
        sides = ((at + 1) % SIDE, (at + 3) % SIDE)
        for d in range(2):
            copies[1, g, h, 0, d] = send(
                acc.at[slab(g, h, d, opposite)], relay1.at[g, h, d], send1.at[g, h, 0, d], recv1.at[g, h, 0, d], h, d
            )
        for d in range(2):
            copies[1, g, h, 1, d] = send(
                acc.at[slab(g, h, 1 - d, sides[d])], direct1.at[g, h, d], send1.at[g, h, 1, d], recv1.at[g, h, 1, d], h, d
            )

    def first_pass_on(g, h):
        at = place[h]
        sides = ((at + 1) % SIDE, (at + 3) % SIDE)
        for d in range(2):
            copies[1, g, h, 0, d].wait_recv()
            own = acc[slab(g, h, d, sides[d])].astype(jnp.float32)
            relay1[g, h, d] = (relay1[g, h, d].astype(jnp.float32) + own).astype(jnp.bfloat16)
            copies[1, g, h, 2, d] = send(
                relay1.at[g, h, d], comb1.at[g, h, d], send1.at[g, h, 2, d], recv1.at[g, h, 2, d], h, d
            )

    def second(g, h):
        at = place[h]
        for d in range(2):
            copies[1, g, h, 1, 1 - d].wait_recv()
            copies[1, g, h, 2, d].wait_recv()
            own = acc[slab(g, h, d, at)].astype(jnp.float32)
            total = own + direct1[g, h, 1 - d].astype(jnp.float32) + comb1[g, h, d].astype(jnp.float32)
            red[g, h, d] = total.astype(jnp.bfloat16)
        axis = 1 - h
        at = place[axis]
        opposite = (at + 2) % SIDE
        sides = ((at + 1) % SIDE, (at + 3) % SIDE)
        for d in range(2):
            copies[2, g, h, 0, d] = send(
                red.at[g, h, d, :, opposite], relay2.at[g, h, d], send2.at[g, h, 0, d], recv2.at[g, h, 0, d], axis, d
            )
        for d in range(2):
            copies[2, g, h, 1, d] = send(
                red.at[g, h, 1 - d, :, sides[d]], direct2.at[g, h, d], send2.at[g, h, 1, d], recv2.at[g, h, 1, d], axis, d
            )

    def second_pass_on(g, h):
        axis = 1 - h
        at = place[axis]
        sides = ((at + 1) % SIDE, (at + 3) % SIDE)
        for d in range(2):
            copies[2, g, h, 0, d].wait_recv()
            own = red[g, h, d, :, sides[d]].astype(jnp.float32)
            relay2[g, h, d] = (relay2[g, h, d].astype(jnp.float32) + own).astype(jnp.bfloat16)
            copies[2, g, h, 2, d] = send(
                relay2.at[g, h, d], comb2.at[g, h, d], send2.at[g, h, 2, d], recv2.at[g, h, 2, d], axis, d
            )

    def finish(g, h):
        at = place[1 - h]
        for d in range(2):
            copies[2, g, h, 1, 1 - d].wait_recv()
            copies[2, g, h, 2, d].wait_recv()
            own = red[g, h, d, :, at].astype(jnp.float32)
            total = own + direct2[g, h, 1 - d].astype(jnp.float32) + comb2[g, h, d].astype(jnp.float32)
            for i in range(2):
                out[GROUPS[g][i], 2 * h + d] = total[i].astype(jnp.bfloat16)

    def both(step, g):
        for h in range(2):
            step(g, h)

    for copy in local:
        copy.wait()
    halos[0].wait_recv()
    halos[1].wait_recv()
    lax.fori_loop(0, 2, lambda i, c: (compute(0, i, 1 + i), c)[1], 0)
    both(first, 0)
    halos[2].wait_recv()
    halos[3].wait_recv()
    compute(1, 0, 0)
    both(first_pass_on, 0)
    compute(1, 1, 3)
    both(first, 1)
    both(second, 0)
    both(first_pass_on, 1)
    both(second_pass_on, 0)
    both(second, 1)
    both(finish, 0)
    both(second_pass_on, 1)
    both(finish, 1)
    for copy in halos + pending:
        copy.wait_send()


def on_device(psi, left_env, right_env, site_ops, coupling, live):
    sec_count, states, width, _ = psi.shape
    row_count = width // lax.axis_size("term")
    anywhere = pl.BlockSpec(memory_space=pl.ANY)
    scalars = pl.BlockSpec(memory_space=pltpu.SMEM)
    bf16 = jnp.bfloat16
    dma = pltpu.SemaphoreType.DMA
    mine = pl.pallas_call(
        functools.partial(kernel, lax.axis_size("sec"), 64),
        out_shape=jax.ShapeDtypeStruct((sec_count, states, row_count, width), bf16),
        in_specs=[anywhere, anywhere, anywhere, scalars, scalars],
        out_specs=pl.BlockSpec(memory_space=pltpu.VMEM),
        scratch_shapes=[
            pltpu.VMEM((6, 4, 256, 256), bf16),
            pltpu.VMEM((2, 4, 256, 256), bf16),
            pltpu.VMEM((4, 256, 1024), bf16),
            pltpu.VMEM((4, 256, 256), bf16),
            pltpu.VMEM((4, 256, 1024), bf16),
            pltpu.VMEM((2, 2, 4, SIDE, SIDE, 16, 256), bf16),
            pltpu.VMEM((2, 2, 2, 2, SIDE, 16, 256), bf16),
            pltpu.VMEM((2, 2, 2, 2, SIDE, 16, 256), bf16),
            pltpu.VMEM((2, 2, 2, 2, SIDE, 16, 256), bf16),
            pltpu.VMEM((2, 2, 2, 2, SIDE, 16, 256), bf16),
            pltpu.VMEM((2, 2, 2, 2, 16, 256), bf16),
            pltpu.VMEM((2, 2, 2, 2, 16, 256), bf16),
            pltpu.VMEM((2, 2, 2, 2, 16, 256), bf16),
            dma((18,)),
            dma((4,)),
            dma((4,)),
            dma((2, 2, 3, 2)),
            dma((2, 2, 3, 2)),
            dma((2, 2, 3, 2)),
            dma((2, 2, 3, 2)),
        ],
        compiler_params=pltpu.CompilerParams(
            collective_id=0, has_side_effects=True, vmem_limit_bytes=48 << 20
        ),
    )(psi, left_env, right_env, site_ops, coupling)
    rows_here = lax.axis_index("term") * row_count + jnp.arange(row_count, dtype=jnp.int32)
    columns = jnp.arange(width, dtype=jnp.int32)
    keep = (rows_here[None, :] < live[:, None])[:, :, None] & (columns[None, :] < live[:, None])[:, None, :]
    return jnp.where(keep[:, None, :, :], mine, jnp.zeros((), bf16))


def solution(mesh):
    placed = (
        P("sec", None, None, None),
        P("term", "sec", None, None),
        P("term", None, None),
        P("term", None, None),
        P("term", "sec"),
        P("sec"),
    )
    return jax.shard_map(
        on_device,
        mesh=mesh,
        in_specs=placed,
        out_specs=P("sec", None, "term", None),
        check_vma=False,
    )
```

time: 192 us -> 56.2 us (0.29)
  the two profiles are of different devices: /device:TPU:2 before, /device:TPU:8 now
where the time goes in v1:
time: 56.2 us; the launch traced here: 55.9 us
  Pallas kernels  48.1 us (86%)
  local copies, waits for them, and re-layouts  5.6 us (10%)
  other arithmetic  2.21 us (4%)
    pallas_call x1, Pallas kernels, on_device(): pl.pallas_call(functools.partial(kernel, lax.axis_size('sec'), 64), out_s...  48.1 us
    unnamed x10, local copies, waits for them, and re-layouts  5.6 us

profile of v1, /device:TPU:8, one launch (start us, length us, event | category | flops | bytes accessed | tf_op | source)
XLA Modules:
  0.0 55.9 jit_solution(4540246820199084676)
XLA Ops:
  0.0 0.7 %broadcast_compare_fusion = pred[4,16]{1,0:T(4,128)(4,1)S(1)} fusion(s32[16]{0:T(128)S(1)} %iota_add_fusion, s32[4]{0:T(128)} %param.11), kind=kLoop, calls=%fused_computation.3 | loop fusion | flops 64 | bytes 144 | tf_op jit(solution)/shard_map/lt | solution.py:257
  0.7 0.7 %iota_compare_fusion = pred[4,256]{1,0:T(4,128)(4,1)S(1)} fusion(s32[4]{0:T(128)} %param.11), kind=kLoop, calls=%fused_computation.2 | loop fusion | flops 1024 | bytes 1040 | tf_op jit(solution)/shard_map/lt | solution.py:257
  1.5 0.1 broadcast_and_fusion
  1.5 0.0 copy-start
  1.6 1.6 %copy-done = bf16[4,4,256,256]{3,2,1,0:T(8,128)(2,1)S(1)} copy-done((bf16[4,4,256,256]{3,2,1,0:T(8,128)(2,1)S(1)}, bf16[4,4,256,256]{3,2,1,0:T(8,128)(2,1)}, u32[]{:S(2)}) %copy-start) | copy-done | bytes 2097176
  3.1 0.0 copy-start.1
  3.1 1.6 %copy-done.1 = bf16[4,4,256,256]{3,2,1,0:T(8,128)(2,1)S(1)} copy-done((bf16[4,4,256,256]{3,2,1,0:T(8,128)(2,1)S(1)}, bf16[4,4,256,256]{3,2,1,0:T(8,128)(2,1)}, u32[]{:S(2)}) %copy-start.1) | copy-done | bytes 2097176
  4.7 0.0 copy-start.2
  4.7 1.0 %copy-done.2 = bf16[4,256,256]{2,1,0:T(8,128)(2,1)S(1)} copy-done((bf16[4,256,256]{2,1,0:T(8,128)(2,1)S(1)}, bf16[4,256,256]{2,1,0:T(8,128)(2,1)}, u32[]{:S(2)}) %copy-start.2) | copy-done | bytes 524312
  5.8 0.0 copy-start.3
  5.8 0.7 %copy-done.3 = f32[4,4,4]{2,1,0:T(4,128)S(1)} copy-done((f32[4,4,4]{2,1,0:T(4,128)S(1)}, f32[4,4,4]{2,1,0:T(4,128)}, u32[]{:S(2)}) %copy-start.3) | copy-done | bytes 280
  6.5 0.0 copy-start.4
  6.5 0.7 %copy-done.4 = s32[4,4]{1,0:T(4,128)S(1)} copy-done((s32[4,4]{1,0:T(4,128)S(1)}, s32[4,4]{1,0:T(4,128)}, u32[]{:S(2)}) %copy-start.4) | copy-done | bytes 88
  7.2 48.1 %shard_map.64 = bf16[4,4,16,256]{3,2,1,0:T(8,128)(2,1)S(1)} custom-call(bf16[4,4,256,256]{3,2,1,0:T(8,128)(2,1)S(1)} %copy-done, bf16[4,4,256,256]{3,2,1,0:T(8,128)(2,1)S(1)} %copy-done.1, bf16[4,256,256]{2,1,0:T(8,128)(2,1)S(1)} %copy-done.2, f32[4,4,4]{2,1,0:T(4,128)S(1)} %copy-done.3, s32[4,4]{1,0:T(4,128)S(1)} %copy-done.4), custom_call_target="tpu_custom_call" | custom-call | tf_op jit(solution)/shard_map/pallas_call | solution.py:224
  55.3 0.7 %broadcast_select_fusion = bf16[4,4,16,256]{3,2,1,0:T(8,128)(2,1)} fusion(bf16[4,4,16,256]{3,2,1,0:T(8,128)(2,1)S(1)} %shard_map.64, pred[4,16,256]{2,1,0:T(8,128)(4,1)S(1)} %broadcast_and_fusion), kind=kLoop, calls=%fused_computation | loop fusion | flops 65536 | bytes 278528 | tf_op jit(solution)/shard_map/jit(_where)/select_n | solution.py:258
  (1 shorter events, 0.0 us)
Async XLA Ops:
  1.5 1.6 %copy-start = (bf16[4,4,256,256]{3,2,1,0:T(8,128)(2,1)S(1)}, bf16[4,4,256,256]{3,2,1,0:T(8,128)(2,1)}, u32[]{:S(2)}) copy-start(bf16[4,4,256,256]{3,2,1,0:T(8,128)(2,1)} %psi.1) | copy-start | bytes 6291460
  3.1 1.6 %copy-start.1 = (bf16[4,4,256,256]{3,2,1,0:T(8,128)(2,1)S(1)}, bf16[4,4,256,256]{3,2,1,0:T(8,128)(2,1)}, u32[]{:S(2)}) copy-start(bf16[4,4,256,256]{3,2,1,0:T(8,128)(2,1)} %left.1) | copy-start | bytes 6291460
  4.7 1.0 %copy-start.2 = (bf16[4,256,256]{2,1,0:T(8,128)(2,1)S(1)}, bf16[4,256,256]{2,1,0:T(8,128)(2,1)}, u32[]{:S(2)}) copy-start(bf16[4,256,256]{2,1,0:T(8,128)(2,1)} %right.1) | copy-start | bytes 1572868
  5.8 0.7 %copy-start.3 = (f32[4,4,4]{2,1,0:T(4,128)S(1)}, f32[4,4,4]{2,1,0:T(4,128)}, u32[]{:S(2)}) copy-start(f32[4,4,4]{2,1,0:T(4,128)} %ops.1) | copy-start | bytes 772
  6.5 0.7 %copy-start.4 = (s32[4,4]{1,0:T(4,128)S(1)}, s32[4,4]{1,0:T(4,128)}, u32[]{:S(2)}) copy-start(s32[4,4]{1,0:T(4,128)} %coupling.1) | copy-start | bytes 196

commit v2 on v0

v2 whole, which is shorter than its diff:
```python
import functools

import jax
import jax.numpy as jnp
from jax import lax
from jax.experimental import pallas as pl
from jax.experimental.pallas import tpu as pltpu
from jax.sharding import PartitionSpec as P

MESH = pl.DeviceIdType.MESH
SIDE = 4
RINGS = (True, True, True, False)
CHUNK = 64


def kernel(
    sections,
    psi, left, right, ops, coupling, live, out,
    held, close, far, lcat, rbuf, ybuf, acc, relay, direct, comb, whole, red, parts,
    local_sem, halo_send, halo_recv, send1, recv1, send2, recv2,
):
    sec = lax.axis_index("sec")
    term = lax.axis_index("term")
    x, y = term % SIDE, term // SIDE
    core = sec % 2
    partner = sec + 1 - 2 * core
    distant = (sec + sections - 1 + 2 * core) % sections
    has_distant = jnp.logical_and(sec > 0, sec < sections - 1)

    def mirror(b):
        return b + core * (3 - 2 * b)

    near = (
        (y * SIDE + (x + 1) % SIDE, y * SIDE + (x + 3) % SIDE, y * SIDE + (x + 2) % SIDE),
        ((y + 1) % SIDE * SIDE + x, (y + 3) % SIDE * SIDE + x, (y + 2) % SIDE * SIDE + x),
    )
    place = (x, y)
    order = [mirror(b) for b in (2, 3, 1, 0)]

    def fetch(n, src, dst):
        copy = pltpu.make_async_copy(src, dst, local_sem.at[n])
        copy.start()
        return copy

    local = [fetch(0, psi, held.at[pl.ds(0, 4)]), fetch(1, right, rbuf)]
    lefts = [fetch(2 + c, left.at[:, order[c]], lcat.at[c]) for c in range(4)]

    def at_sec(other):
        return {"sec": other, "term": term}

    def at_term(other):
        return {"sec": sec, "term": other}

    barrier = pltpu.get_barrier_semaphore()
    pl.semaphore_signal(barrier, inc=1, device_id=at_sec(partner), device_id_type=MESH)

    @pl.when(has_distant)
    def _():
        pl.semaphore_signal(barrier, inc=1, device_id=at_sec(distant), device_id_type=MESH)

    for axis in range(2):
        for d in range(3):
            pl.semaphore_signal(barrier, inc=1, device_id=at_term(near[axis][d]), device_id_type=MESH)
    pl.semaphore_wait(barrier, 7 + has_distant.astype(jnp.int32))

    def halo(n, src, dst, other):
        return pltpu.make_async_remote_copy(
            src_ref=src, dst_ref=dst, send_sem=halo_send.at[n], recv_sem=halo_recv.at[n],
            device_id=at_sec(other), device_id_type=MESH,
        )

    halos = [
        halo(0, psi.at[mirror(0)], close, distant),
        halo(1, psi.at[mirror(1)], far, distant),
        halo(2, psi.at[mirror(3)], held.at[4], partner),
        halo(3, psi.at[mirror(2)], held.at[5], partner),
    ]

    @pl.when(has_distant)
    def _():
        halos[0].start()
        halos[1].start()

    halos[2].start()
    halos[3].start()

    def compute(c):
        s = order[c]
        for t in range(4):
            target = coupling[t, s]
            valid = target >= 0
            block = target - sec * 4
            seen = mirror(block)
            own = jnp.logical_and(block >= 0, block < 4)
            index = jnp.where(own, block, jnp.where(seen == 4, 4, 5))
            coef = [
                [jnp.where(valid, ops[t, k, j], 0.0).astype(jnp.bfloat16) for j in range(4)] for k in range(4)
            ]
            weights = rbuf[t]
            for r in range(0, 256, CHUNK):
                rows = pl.ds(r, CHUNK)
                source = []
                for j in range(4):
                    value = held[index, j, rows, :]
                    if c >= 2:
                        value = jnp.where(seen == -1, close[j, rows, :], value)
                    if c == 3:
                        value = jnp.where(seen == -2, far[j, rows, :], value)
                    source.append(value)
                mixed = []
                for k in range(4):
                    total = coef[k][0] * source[0]
                    for j in range(1, 4):
                        total = total + coef[k][j] * source[j]
                    mixed.append(total)
                inner = jnp.dot(
                    jnp.concatenate(mixed, axis=0), weights, preferred_element_type=jnp.float32
                ).astype(jnp.bfloat16)
                for k in range(4):
                    ybuf[t, rows, pl.ds(256 * k, 256)] = inner[k * CHUNK : (k + 1) * CHUNK]
        for k in range(4):
            total = None
            for t in range(4):
                term_part = jnp.dot(
                    lcat[c, t], ybuf[t, :, pl.ds(256 * k, 256)], preferred_element_type=jnp.float32
                )
                total = term_part if total is None else total + term_part
            acc[c, k] = total.astype(jnp.bfloat16).reshape(SIDE, SIDE, 16, 256)

    pending = []
    copies = {}

    def send(src, dst, send_sem, recv_sem, axis, direction):
        copy = pltpu.make_async_remote_copy(
            src_ref=src, dst_ref=dst, send_sem=send_sem, recv_sem=recv_sem,
            device_id=at_term(near[axis][direction]), device_id_type=MESH,
        )
        copy.start()
        pending.append(copy)
        return copy

    def targets(axis):
        at = place[axis]
        return ((at + 1) % SIDE, (at + 3) % SIDE, (at + 2) % SIDE)

    def slab(c, h, d, at):
        return (c, 2 * h + d, slice(None), at) if h == 0 else (c, 2 * h + d, at)

    def pair(c, h, at):
        return (c, pl.ds(2 * h, 2), slice(None), at) if h == 0 else (c, pl.ds(2 * h, 2), at)

    def first(c):
        for h in range(2):
            goal = targets(h)
            if RINGS[c]:
                for d in range(2):
                    copies[1, c, h, 0, d] = send(
                        acc.at[slab(c, h, d, goal[2])], relay.at[c, h, d],
                        send1.at[c, h, 0, d], recv1.at[c, h, 0, d], h, d,
                    )
                for d in range(2):
                    copies[1, c, h, 1, d] = send(
                        acc.at[slab(c, h, 1 - d, goal[d])], direct.at[c, h, d],
                        send1.at[c, h, 1, d], recv1.at[c, h, 1, d], h, d,
                    )
            else:
                for d in (2, 0, 1):
                    copies[1, c, h, d] = send(
                        acc.at[pair(c, h, goal[d])], whole.at[h, d],
                        send1.at[c, h, d, 0], recv1.at[c, h, d, 0], h, d,
                    )

    def pass_on(c):
        for h in range(2):
            goal = targets(h)
            for d in range(2):
                copies[1, c, h, 0, d].wait_recv()
                own = acc[slab(c, h, d, goal[d])].astype(jnp.float32)
                relay[c, h, d] = (relay[c, h, d].astype(jnp.float32) + own).astype(jnp.bfloat16)
                copies[1, c, h, 2, d] = send(
                    relay.at[c, h, d], comb.at[c, h, d], send1.at[c, h, 2, d], recv1.at[c, h, 2, d], h, d
                )

    def second(c):
        for h in range(2):
            if RINGS[c]:
                for d in range(2):
                    copies[1, c, h, 1, 1 - d].wait_recv()
                    copies[1, c, h, 2, d].wait_recv()
                    total = acc[slab(c, h, d, place[h])].astype(jnp.float32)
                    total = total + direct[c, h, 1 - d].astype(jnp.float32) + comb[c, h, d].astype(jnp.float32)
                    red[c, h, d] = total.astype(jnp.bfloat16)
            else:
                total = acc[pair(c, h, place[h])].astype(jnp.float32)
                for d in range(3):
                    copies[1, c, h, d].wait_recv()
                    total = total + whole[h, d].astype(jnp.float32)
                red[c, h] = total.astype(jnp.bfloat16)
            goal = targets(1 - h)
            for d in (2, 0, 1):
                copies[2, c, h, d] = send(
                    red.at[c, h, :, goal[d]], parts.at[c, h, d], send2.at[c, h, d], recv2.at[c, h, d], 1 - h, d
                )

    row = term * 16 + lax.broadcasted_iota(jnp.int32, (2, 16, 256), 1)
    column = lax.broadcasted_iota(jnp.int32, (2, 16, 256), 2)
    furthest = jnp.maximum(row, column)

    def finish(c):
        s = order[c]
        for h in range(2):
            total = red[c, h, :, place[1 - h]].astype(jnp.float32)
            for d in range(3):
                copies[2, c, h, d].wait_recv()
                total = total + parts[c, h, d].astype(jnp.float32)
            out[s, pl.ds(2 * h, 2)] = jnp.where(furthest < live[s], total, 0.0).astype(jnp.bfloat16)

    for copy in local:
        copy.wait()
    halos[2].wait_recv()
    halos[3].wait_recv()
    lefts[0].wait()
    compute(0)
    first(0)
    lefts[1].wait()
    compute(1)
    first(1)
    pass_on(0)

    @pl.when(has_distant)
    def _():
        halos[0].wait_recv()

    lefts[2].wait()
    compute(2)
    first(2)
    pass_on(1)
    second(0)
    pass_on(2)
    second(1)

    @pl.when(has_distant)
    def _():
        halos[1].wait_recv()

    lefts[3].wait()
    compute(3)
    first(3)
    second(2)
    finish(0)
    finish(1)
    second(3)
    finish(2)
    finish(3)

    @pl.when(has_distant)
    def _():
        halos[0].wait_send()
        halos[1].wait_send()

    for copy in halos[2:] + pending:
        copy.wait_send()


def on_device(psi, left_env, right_env, site_ops, coupling, live):
    sec_count, states, width, _ = psi.shape
    row_count = width // lax.axis_size("term")
    anywhere = pl.BlockSpec(memory_space=pl.ANY)
    scalars = pl.BlockSpec(memory_space=pltpu.SMEM)
    bf16 = jnp.bfloat16
    dma = pltpu.SemaphoreType.DMA
    return pl.pallas_call(
        functools.partial(kernel, lax.axis_size("sec")),
        out_shape=jax.ShapeDtypeStruct((sec_count, states, row_count, width), bf16),
        in_specs=[anywhere, anywhere, anywhere, scalars, scalars, scalars],
        out_specs=pl.BlockSpec(memory_space=pltpu.VMEM),
        scratch_shapes=[
            pltpu.VMEM((6, 4, 256, 256), bf16),
            pltpu.VMEM((4, 256, 256), bf16),
            pltpu.VMEM((4, 256, 256), bf16),
            pltpu.VMEM((4, 4, 256, 256), bf16),
            pltpu.VMEM((4, 256, 256), bf16),
            pltpu.VMEM((4, 256, 1024), bf16),
            pltpu.VMEM((4, 4, SIDE, SIDE, 16, 256), bf16),
            pltpu.VMEM((4, 2, 2, SIDE, 16, 256), bf16),
            pltpu.VMEM((4, 2, 2, SIDE, 16, 256), bf16),
            pltpu.VMEM((4, 2, 2, SIDE, 16, 256), bf16),
            pltpu.VMEM((2, 3, 2, SIDE, 16, 256), bf16),
            pltpu.VMEM((4, 2, 2, SIDE, 16, 256), bf16),
            pltpu.VMEM((4, 2, 3, 2, 16, 256), bf16),
            dma((6,)),
            dma((4,)),
            dma((4,)),
            dma((4, 2, 3, 2)),
            dma((4, 2, 3, 2)),
            dma((4, 2, 3)),
            dma((4, 2, 3)),
        ],
        compiler_params=pltpu.CompilerParams(
            collective_id=0, has_side_effects=True, vmem_limit_bytes=63 << 20
        ),
    )(psi, left_env, right_env, site_ops, coupling, live)


def solution(mesh):
    placed = (
        P("sec", None, None, None),
        P("term", "sec", None, None),
        P("term", None, None),
        P("term", None, None),
        P("term", "sec"),
        P("sec"),
    )
    return jax.shard_map(
        on_device,
        mesh=mesh,
        in_specs=placed,
        out_specs=P("sec", None, "term", None),
        check_vma=False,
    )
```

time: 192 us -> 36.2 us (0.19)
  the two profiles are of different devices: /device:TPU:2 before, /device:TPU:225 now
where the time goes in v2:
time: 36.2 us; the launch traced here: 36 us
  Pallas kernels  34.4 us (95%)
  local copies, waits for them, and re-layouts  1.57 us (4%)
    pallas_call x1, Pallas kernels, on_device(): pl.pallas_call(functools.partial(kernel, lax.axis_size('sec')), out_shape...  34.4 us
    unnamed x1, local copies, waits for them, and re-layouts  1.57 us

profile of v2, /device:TPU:225, one launch (start us, length us, event | category | flops | bytes accessed | tf_op | source)
XLA Modules:
  0.0 36.0 jit_solution(12842082818740452641)
XLA Ops:
  0.0 34.4 %shard_map.64 = bf16[4,4,16,256]{3,2,1,0:T(8,128)(2,1)} custom-call(bf16[4,4,256,256]{3,2,1,0:T(8,128)(2,1)} %psi.1, bf16[4,4,256,256]{3,2,1,0:T(8,128)(2,1)} %left.1, bf16[4,256,256]{2,1,0:T(8,128)(2,1)} %right.1, f32[4,4,4]{2,1,0:T(4,128)} %ops.1, s32[4,4]{1,0:T(4,128)} %coupling.1, s32[4]{0:T(128)} %live.1), custom_call_target="tpu_custom_call" | custom-call | tf_op jit(solution)/shard_map/pallas_call | solution.py:272
  34.4 1.6 %copy.8 = bf16[4,4,16,256]{3,2,1,0:T(8,128)(2,1)} copy(bf16[4,4,16,256]{3,2,1,0:T(8,128)(2,1)} %shard_map.64) | data formatting | bytes 262144

commit v3 on v2

--- a/solution.py
+++ b/solution.py
@@ -9,15 +9,14 @@
 
 MESH = pl.DeviceIdType.MESH
 SIDE = 4
-RINGS = (True, True, True, False)
 CHUNK = 64
 
 
 def kernel(
     sections,
     psi, left, right, ops, coupling, live, out,
-    held, close, far, lcat, rbuf, ybuf, acc, relay, direct, comb, whole, red, parts,
-    local_sem, halo_send, halo_recv, send1, recv1, send2, recv2,
+    held, after, close, far, lcat, rbuf, ybuf, acc, relay, direct, comb, red, parts,
+    local_sem, halo_send, halo_recv, share_send, share_recv, send1, recv1, send2, recv2,
 ):
     sec = lax.axis_index("sec")
     term = lax.axis_index("term")
@@ -69,11 +68,20 @@
             device_id=at_sec(other), device_id_type=MESH,
         )
 
+    mine = x + core * (y - x)
+    theirs = y + core * (x - y)
     halos = [
-        halo(0, psi.at[mirror(0)], close, distant),
-        halo(1, psi.at[mirror(1)], far, distant),
+        halo(0, psi.at[mirror(1), theirs], far.at[theirs], distant),
+        halo(1, psi.at[mirror(0)], close, distant),
         halo(2, psi.at[mirror(3)], held.at[4], partner),
-        halo(3, psi.at[mirror(2)], held.at[5], partner),
+        halo(3, psi.at[mirror(2)], after, partner),
+    ]
+    shares = [
+        pltpu.make_async_remote_copy(
+            src_ref=far.at[mine], dst_ref=far.at[mine], send_sem=share_send.at[d], recv_sem=share_recv.at[d],
+            device_id=at_term(near[0][d] + core * (near[1][d] - near[0][d])), device_id_type=MESH,
+        )
+        for d in range(3)
     ]
 
     @pl.when(has_distant)
@@ -89,10 +97,10 @@
         for t in range(4):
             target = coupling[t, s]
             valid = target >= 0
-            block = target - sec * 4
+            block = jnp.where(valid, target - sec * 4, 0)
             seen = mirror(block)
             own = jnp.logical_and(block >= 0, block < 4)
-            index = jnp.where(own, block, jnp.where(seen == 4, 4, 5))
+            index = jnp.where(own, block, 4)
             coef = [
                 [jnp.where(valid, ops[t, k, j], 0.0).astype(jnp.bfloat16) for j in range(4)] for k in range(4)
             ]
@@ -102,6 +110,8 @@
                 source = []
                 for j in range(4):
                     value = held[index, j, rows, :]
+                    if c == 1:
+                        value = jnp.where(seen == 5, after[j, rows, :], value)
                     if c >= 2:
                         value = jnp.where(seen == -1, close[j, rows, :], value)
                     if c == 3:
@@ -146,29 +156,19 @@
     def slab(c, h, d, at):
         return (c, 2 * h + d, slice(None), at) if h == 0 else (c, 2 * h + d, at)
 
-    def pair(c, h, at):
-        return (c, pl.ds(2 * h, 2), slice(None), at) if h == 0 else (c, pl.ds(2 * h, 2), at)
-
     def first(c):
         for h in range(2):
             goal = targets(h)
-            if RINGS[c]:
-                for d in range(2):
-                    copies[1, c, h, 0, d] = send(
-                        acc.at[slab(c, h, d, goal[2])], relay.at[c, h, d],
-                        send1.at[c, h, 0, d], recv1.at[c, h, 0, d], h, d,
-                    )
-                for d in range(2):
-                    copies[1, c, h, 1, d] = send(
-                        acc.at[slab(c, h, 1 - d, goal[d])], direct.at[c, h, d],
-                        send1.at[c, h, 1, d], recv1.at[c, h, 1, d], h, d,
-                    )
-            else:
-                for d in (2, 0, 1):
-                    copies[1, c, h, d] = send(
-                        acc.at[pair(c, h, goal[d])], whole.at[h, d],
-                        send1.at[c, h, d, 0], recv1.at[c, h, d, 0], h, d,
-                    )
+            for d in range(2):
+                copies[1, c, h, 0, d] = send(
+                    acc.at[slab(c, h, d, goal[2])], relay.at[c, h, d],
+                    send1.at[c, h, 0, d], recv1.at[c, h, 0, d], h, d,
+                )
+            for d in range(2):
+                copies[1, c, h, 1, d] = send(
+                    acc.at[slab(c, h, 1 - d, goal[d])], direct.at[c, h, d],
+                    send1.at[c, h, 1, d], recv1.at[c, h, 1, d], h, d,
+                )
 
     def pass_on(c):
         for h in range(2):
@@ -183,19 +183,12 @@
 
     def second(c):
         for h in range(2):
-            if RINGS[c]:
-                for d in range(2):
-                    copies[1, c, h, 1, 1 - d].wait_recv()
-                    copies[1, c, h, 2, d].wait_recv()
-                    total = acc[slab(c, h, d, place[h])].astype(jnp.float32)
-                    total = total + direct[c, h, 1 - d].astype(jnp.float32) + comb[c, h, d].astype(jnp.float32)
-                    red[c, h, d] = total.astype(jnp.bfloat16)
-            else:
-                total = acc[pair(c, h, place[h])].astype(jnp.float32)
-                for d in range(3):
-                    copies[1, c, h, d].wait_recv()
-                    total = total + whole[h, d].astype(jnp.float32)
-                red[c, h] = total.astype(jnp.bfloat16)
+            for d in range(2):
+                copies[1, c, h, 1, 1 - d].wait_recv()
+                copies[1, c, h, 2, d].wait_recv()
+                total = acc[slab(c, h, d, place[h])].astype(jnp.float32)
+                total = total + direct[c, h, 1 - d].astype(jnp.float32) + comb[c, h, d].astype(jnp.float32)
+                red[c, h, d] = total.astype(jnp.bfloat16)
             goal = targets(1 - h)
             for d in (2, 0, 1):
                 copies[2, c, h, d] = send(
@@ -218,45 +211,54 @@
     for copy in local:
         copy.wait()
     halos[2].wait_recv()
-    halos[3].wait_recv()
+
+    @pl.when(has_distant)
+    def _():
+        halos[0].wait_recv()
+        for copy in shares:
+            copy.start()
+
     lefts[0].wait()
     compute(0)
     first(0)
     lefts[1].wait()
+    halos[3].wait_recv()
     compute(1)
     first(1)
-    pass_on(0)
-
-    @pl.when(has_distant)
-    def _():
-        halos[0].wait_recv()
+
+    @pl.when(has_distant)
+    def _():
+        halos[1].wait_recv()
 
     lefts[2].wait()
     compute(2)
     first(2)
+    pass_on(0)
     pass_on(1)
-    second(0)
-    pass_on(2)
-    second(1)
-
-    @pl.when(has_distant)
-    def _():
-        halos[1].wait_recv()
+
+    @pl.when(has_distant)
+    def _():
+        for copy in shares:
+            copy.wait_recv()
 
     lefts[3].wait()
     compute(3)
     first(3)
+    pass_on(2)
+    pass_on(3)
+    second(0)
+    second(1)
     second(2)
+    second(3)
     finish(0)
     finish(1)
-    second(3)
     finish(2)
     finish(3)
 
     @pl.when(has_distant)
     def _():
-        halos[0].wait_send()
-        halos[1].wait_send()
+        for copy in halos[:2] + shares:
+            copy.wait_send()
 
     for copy in halos[2:] + pending:
         copy.wait_send()
@@ -275,7 +277,8 @@
         in_specs=[anywhere, anywhere, anywhere, scalars, scalars, scalars],
         out_specs=pl.BlockSpec(memory_space=pltpu.VMEM),
         scratch_shapes=[
-            pltpu.VMEM((6, 4, 256, 256), bf16),
+            pltpu.VMEM((5, 4, 256, 256), bf16),
+            pltpu.VMEM((4, 256, 256), bf16),
             pltpu.VMEM((4, 256, 256), bf16),
             pltpu.VMEM((4, 256, 256), bf16),
             pltpu.VMEM((4, 4, 256, 256), bf16),
@@ -285,12 +288,13 @@
             pltpu.VMEM((4, 2, 2, SIDE, 16, 256), bf16),
             pltpu.VMEM((4, 2, 2, SIDE, 16, 256), bf16),
             pltpu.VMEM((4, 2, 2, SIDE, 16, 256), bf16),
-            pltpu.VMEM((2, 3, 2, SIDE, 16, 256), bf16),
             pltpu.VMEM((4, 2, 2, SIDE, 16, 256), bf16),
             pltpu.VMEM((4, 2, 3, 2, 16, 256), bf16),
             dma((6,)),
             dma((4,)),
             dma((4,)),
+            dma((3,)),
+            dma((3,)),
             dma((4, 2, 3, 2)),
             dma((4, 2, 3, 2)),
             dma((4, 2, 3)),

time: 36.2 us -> 35.1 us (0.970)
  the two profiles are of different devices: /device:TPU:225 before, /device:TPU:384 now
where the time goes in v3:
time: 35.1 us; the launch traced here: 34.9 us
  Pallas kernels  33.4 us (95%)
  local copies, waits for them, and re-layouts  1.57 us (4%)
    pallas_call x1, Pallas kernels, on_device(): pl.pallas_call(functools.partial(kernel, lax.axis_size('sec')), out_shape...  33.4 us
    unnamed x1, local copies, waits for them, and re-layouts  1.57 us

profile of v3, /device:TPU:384, one launch (start us, length us, event | category | flops | bytes accessed | tf_op | source)
XLA Modules:
  0.0 34.9 jit_solution(12356697134460187977)
XLA Ops:
  0.0 33.4 %shard_map.64 = bf16[4,4,16,256]{3,2,1,0:T(8,128)(2,1)} custom-call(bf16[4,4,256,256]{3,2,1,0:T(8,128)(2,1)} %psi.1, bf16[4,4,256,256]{3,2,1,0:T(8,128)(2,1)} %left.1, bf16[4,256,256]{2,1,0:T(8,128)(2,1)} %right.1, f32[4,4,4]{2,1,0:T(4,128)} %ops.1, s32[4,4]{1,0:T(4,128)} %coupling.1, s32[4]{0:T(128)} %live.1), custom_call_target="tpu_custom_call" | custom-call | tf_op jit(solution)/shard_map/pallas_call | solution.py:274
  33.4 1.6 %copy.8 = bf16[4,4,16,256]{3,2,1,0:T(8,128)(2,1)} copy(bf16[4,4,16,256]{3,2,1,0:T(8,128)(2,1)} %shard_map.64) | data formatting | bytes 262144

commit v4 on v3

--- a/solution.py
+++ b/solution.py
@@ -16,7 +16,7 @@
     sections,
     psi, left, right, ops, coupling, live, out,
     held, after, close, far, lcat, rbuf, ybuf, acc, relay, direct, comb, red, parts,
-    local_sem, halo_send, halo_recv, share_send, share_recv, send1, recv1, send2, recv2,
+    local_sem, halo_send, halo_recv, share_send, share_recv, send1, recv1, sendc, recvc, send2, recv2,
 ):
     sec = lax.axis_index("sec")
     term = lax.axis_index("term")
@@ -70,27 +70,37 @@
 
     mine = x + core * (y - x)
     theirs = y + core * (x - y)
+
+    def piece(q):
+        return (0, pl.ds(pl.multiple_of(q * 64, 64), 64))
+
     halos = [
-        halo(0, psi.at[mirror(1), theirs], far.at[theirs], distant),
-        halo(1, psi.at[mirror(0)], close, distant),
-        halo(2, psi.at[mirror(3)], held.at[4], partner),
-        halo(3, psi.at[mirror(2)], after, partner),
+        halo(0, psi.at[(mirror(0),) + piece(theirs)], close.at[piece(theirs)], distant),
+        halo(1, psi.at[(mirror(1),) + piece(theirs)], far.at[piece(theirs)], distant),
+        halo(2, psi.at[mirror(0), pl.ds(1, 3)], close.at[pl.ds(1, 3)], distant),
+        halo(3, psi.at[mirror(1), pl.ds(1, 3)], far.at[pl.ds(1, 3)], distant),
+        halo(4, psi.at[mirror(3)], held.at[4], partner),
+        halo(5, psi.at[mirror(2)], after, partner),
     ]
     shares = [
-        pltpu.make_async_remote_copy(
-            src_ref=far.at[mine], dst_ref=far.at[mine], send_sem=share_send.at[d], recv_sem=share_recv.at[d],
-            device_id=at_term(near[0][d] + core * (near[1][d] - near[0][d])), device_id_type=MESH,
-        )
-        for d in range(3)
+        [
+            pltpu.make_async_remote_copy(
+                src_ref=block.at[piece(mine)], dst_ref=block.at[piece(mine)],
+                send_sem=share_send.at[n, d], recv_sem=share_recv.at[n, d],
+                device_id=at_term(near[0][d] + core * (near[1][d] - near[0][d])), device_id_type=MESH,
+            )
+            for d in range(3)
+        ]
+        for n, block in enumerate((close, far))
     ]
 
     @pl.when(has_distant)
     def _():
-        halos[0].start()
-        halos[1].start()
-
-    halos[2].start()
-    halos[3].start()
+        for copy in halos[:3]:
+            copy.start()
+
+    halos[4].start()
+    halos[5].start()
 
     def compute(c):
         s = order[c]
@@ -157,111 +167,122 @@
         return (c, 2 * h + d, slice(None), at) if h == 0 else (c, 2 * h + d, at)
 
     def first(c):
+        g, i = c // 2, c % 2
         for h in range(2):
             goal = targets(h)
             for d in range(2):
-                copies[1, c, h, 0, d] = send(
-                    acc.at[slab(c, h, d, goal[2])], relay.at[c, h, d],
+                copies[0, c, h, d] = send(
+                    acc.at[slab(c, h, d, goal[2])], relay.at[g, h, d, i],
                     send1.at[c, h, 0, d], recv1.at[c, h, 0, d], h, d,
                 )
             for d in range(2):
-                copies[1, c, h, 1, d] = send(
-                    acc.at[slab(c, h, 1 - d, goal[d])], direct.at[c, h, d],
+                copies[1, c, h, d] = send(
+                    acc.at[slab(c, h, 1 - d, goal[d])], direct.at[g, h, d, i],
                     send1.at[c, h, 1, d], recv1.at[c, h, 1, d], h, d,
                 )
 
-    def pass_on(c):
+    def pass_on(g):
+        blocks = pl.ds(2 * g, 2)
         for h in range(2):
             goal = targets(h)
             for d in range(2):
-                copies[1, c, h, 0, d].wait_recv()
-                own = acc[slab(c, h, d, goal[d])].astype(jnp.float32)
-                relay[c, h, d] = (relay[c, h, d].astype(jnp.float32) + own).astype(jnp.bfloat16)
-                copies[1, c, h, 2, d] = send(
-                    relay.at[c, h, d], comb.at[c, h, d], send1.at[c, h, 2, d], recv1.at[c, h, 2, d], h, d
-                )
-
-    def second(c):
+                for i in range(2):
+                    copies[0, 2 * g + i, h, d].wait_recv()
+                own = acc[slab(blocks, h, d, goal[d])].astype(jnp.float32)
+                relay[g, h, d] = (relay[g, h, d].astype(jnp.float32) + own).astype(jnp.bfloat16)
+                copies[2, g, h, d] = send(
+                    relay.at[g, h, d], comb.at[g, h, d], sendc.at[g, h, d], recvc.at[g, h, d], h, d
+                )
+
+    def second(g):
+        blocks = pl.ds(2 * g, 2)
         for h in range(2):
             for d in range(2):
-                copies[1, c, h, 1, 1 - d].wait_recv()
-                copies[1, c, h, 2, d].wait_recv()
-                total = acc[slab(c, h, d, place[h])].astype(jnp.float32)
-                total = total + direct[c, h, 1 - d].astype(jnp.float32) + comb[c, h, d].astype(jnp.float32)
-                red[c, h, d] = total.astype(jnp.bfloat16)
+                for i in range(2):
+                    copies[1, 2 * g + i, h, 1 - d].wait_recv()
+                copies[2, g, h, d].wait_recv()
+                total = acc[slab(blocks, h, d, place[h])].astype(jnp.float32)
+                total = total + direct[g, h, 1 - d].astype(jnp.float32) + comb[g, h, d].astype(jnp.float32)
+                red[g, h, d] = total.astype(jnp.bfloat16)
             goal = targets(1 - h)
             for d in (2, 0, 1):
-                copies[2, c, h, d] = send(
-                    red.at[c, h, :, goal[d]], parts.at[c, h, d], send2.at[c, h, d], recv2.at[c, h, d], 1 - h, d
-                )
+                copies[3, g, h, d] = send(
+                    red.at[g, h, :, :, goal[d]], parts.at[g, h, d], send2.at[g, h, d], recv2.at[g, h, d], 1 - h, d
+                )
+
+    def sent():
+        while pending:
+            pending.pop().wait_send()
 
     row = term * 16 + lax.broadcasted_iota(jnp.int32, (2, 16, 256), 1)
     column = lax.broadcasted_iota(jnp.int32, (2, 16, 256), 2)
     furthest = jnp.maximum(row, column)
 
-    def finish(c):
-        s = order[c]
+    def finish(g):
         for h in range(2):
-            total = red[c, h, :, place[1 - h]].astype(jnp.float32)
+            total = red[g, h, :, :, place[1 - h]].astype(jnp.float32)
             for d in range(3):
-                copies[2, c, h, d].wait_recv()
-                total = total + parts[c, h, d].astype(jnp.float32)
-            out[s, pl.ds(2 * h, 2)] = jnp.where(furthest < live[s], total, 0.0).astype(jnp.bfloat16)
+                copies[3, g, h, d].wait_recv()
+                total = total + parts[g, h, d].astype(jnp.float32)
+            for i in range(2):
+                s = order[2 * g + i]
+                out[s, pl.ds(2 * h, 2)] = jnp.where(furthest < live[s], total[:, i], 0.0).astype(jnp.bfloat16)
 
     for copy in local:
         copy.wait()
-    halos[2].wait_recv()
-
-    @pl.when(has_distant)
-    def _():
-        halos[0].wait_recv()
-        for copy in shares:
-            copy.start()
+    halos[4].wait_recv()
+
+    @pl.when(has_distant)
+    def _():
+        for n in range(2):
+            halos[n].wait_recv()
+            for copy in shares[n]:
+                copy.start()
+        halos[3].start()
 
     lefts[0].wait()
     compute(0)
     first(0)
+
     lefts[1].wait()
-    halos[3].wait_recv()
+    halos[5].wait_recv()
     compute(1)
     first(1)
 
     @pl.when(has_distant)
     def _():
-        halos[1].wait_recv()
+        halos[2].wait_recv()
+        for copy in shares[0]:
+            copy.wait_recv()
 
     lefts[2].wait()
     compute(2)
     first(2)
     pass_on(0)
-    pass_on(1)
-
-    @pl.when(has_distant)
-    def _():
-        for copy in shares:
+
+    @pl.when(has_distant)
+    def _():
+        halos[3].wait_recv()
+        for copy in shares[1]:
             copy.wait_recv()
 
     lefts[3].wait()
     compute(3)
     first(3)
-    pass_on(2)
-    pass_on(3)
     second(0)
+    pass_on(1)
     second(1)
-    second(2)
-    second(3)
+
+    @pl.when(has_distant)
+    def _():
+        for copy in halos[:4] + shares[0] + shares[1]:
+            copy.wait_send()
+
+    halos[4].wait_send()
+    halos[5].wait_send()
     finish(0)
     finish(1)
-    finish(2)
-    finish(3)
-
-    @pl.when(has_distant)
-    def _():
-        for copy in halos[:2] + shares:
-            copy.wait_send()
-
-    for copy in halos[2:] + pending:
-        copy.wait_send()
+    sent()
 
 
 def on_device(psi, left_env, right_env, site_ops, coupling, live):
@@ -285,20 +306,22 @@
             pltpu.VMEM((4, 256, 256), bf16),
             pltpu.VMEM((4, 256, 1024), bf16),
             pltpu.VMEM((4, 4, SIDE, SIDE, 16, 256), bf16),
-            pltpu.VMEM((4, 2, 2, SIDE, 16, 256), bf16),
-            pltpu.VMEM((4, 2, 2, SIDE, 16, 256), bf16),
-            pltpu.VMEM((4, 2, 2, SIDE, 16, 256), bf16),
-            pltpu.VMEM((4, 2, 2, SIDE, 16, 256), bf16),
-            pltpu.VMEM((4, 2, 3, 2, 16, 256), bf16),
+            pltpu.VMEM((2, 2, 2, 2, SIDE, 16, 256), bf16),
+            pltpu.VMEM((2, 2, 2, 2, SIDE, 16, 256), bf16),
+            pltpu.VMEM((2, 2, 2, 2, SIDE, 16, 256), bf16),
+            pltpu.VMEM((2, 2, 2, 2, SIDE, 16, 256), bf16),
+            pltpu.VMEM((2, 2, 3, 2, 2, 16, 256), bf16),
             dma((6,)),
-            dma((4,)),
-            dma((4,)),
-            dma((3,)),
-            dma((3,)),
-            dma((4, 2, 3, 2)),
-            dma((4, 2, 3, 2)),
-            dma((4, 2, 3)),
-            dma((4, 2, 3)),
+            dma((6,)),
+            dma((6,)),
+            dma((2, 3)),
+            dma((2, 3)),
+            dma((4, 2, 2, 2)),
+            dma((4, 2, 2, 2)),
+            dma((2, 2, 2)),
+            dma((2, 2, 2)),
+            dma((2, 2, 3)),
+            dma((2, 2, 3)),
         ],
         compiler_params=pltpu.CompilerParams(
             collective_id=0, has_side_effects=True, vmem_limit_bytes=63 << 20

time: 35.1 us -> 34.9 us (level)
  no operation moved by 1% of the time
where the time goes in v4:
time: 34.9 us; the launch traced here: 34.8 us
  Pallas kernels  33.2 us (95%)
  local copies, waits for them, and re-layouts  1.57 us (4%)
    pallas_call x1, Pallas kernels, on_device(): pl.pallas_call(functools.partial(kernel, lax.axis_size('sec')), out_shape...  33.2 us
    unnamed x1, local copies, waits for them, and re-layouts  1.57 us

profile of v4, /device:TPU:384, one launch (start us, length us, event | category | flops | bytes accessed | tf_op | source)
XLA Modules:
  0.0 34.8 jit_solution(15242316445237311313)
XLA Ops:
  0.0 33.2 %shard_map.64 = bf16[4,4,16,256]{3,2,1,0:T(8,128)(2,1)} custom-call(bf16[4,4,256,256]{3,2,1,0:T(8,128)(2,1)} %psi.1, bf16[4,4,256,256]{3,2,1,0:T(8,128)(2,1)} %left.1, bf16[4,256,256]{2,1,0:T(8,128)(2,1)} %right.1, f32[4,4,4]{2,1,0:T(4,128)} %ops.1, s32[4,4]{1,0:T(4,128)} %coupling.1, s32[4]{0:T(128)} %live.1), custom_call_target="tpu_custom_call" | custom-call | tf_op jit(solution)/shard_map/pallas_call | solution.py:295
  33.2 1.6 %copy.8 = bf16[4,4,16,256]{3,2,1,0:T(8,128)(2,1)} copy(bf16[4,4,16,256]{3,2,1,0:T(8,128)(2,1)} %shard_map.64) | data formatting | bytes 262144

commit v5 on v4

--- a/solution.py
+++ b/solution.py
@@ -146,6 +146,8 @@
                 )
                 total = term_part if total is None else total + term_part
             acc[c, k] = total.astype(jnp.bfloat16).reshape(SIDE, SIDE, 16, 256)
+            if k % 2:
+                first(c, k // 2)
 
     pending = []
     copies = {}
@@ -166,20 +168,19 @@
     def slab(c, h, d, at):
         return (c, 2 * h + d, slice(None), at) if h == 0 else (c, 2 * h + d, at)
 
-    def first(c):
+    def first(c, h):
         g, i = c // 2, c % 2
-        for h in range(2):
-            goal = targets(h)
-            for d in range(2):
-                copies[0, c, h, d] = send(
-                    acc.at[slab(c, h, d, goal[2])], relay.at[g, h, d, i],
-                    send1.at[c, h, 0, d], recv1.at[c, h, 0, d], h, d,
-                )
-            for d in range(2):
-                copies[1, c, h, d] = send(
-                    acc.at[slab(c, h, 1 - d, goal[d])], direct.at[g, h, d, i],
-                    send1.at[c, h, 1, d], recv1.at[c, h, 1, d], h, d,
-                )
+        goal = targets(h)
+        for d in range(2):
+            copies[0, c, h, d] = send(
+                acc.at[slab(c, h, d, goal[2])], relay.at[g, h, d, i],
+                send1.at[c, h, 0, d], recv1.at[c, h, 0, d], h, d,
+            )
+        for d in range(2):
+            copies[1, c, h, d] = send(
+                acc.at[slab(c, h, 1 - d, goal[d])], direct.at[g, h, d, i],
+                send1.at[c, h, 1, d], recv1.at[c, h, 1, d], h, d,
+            )
 
     def pass_on(g):
         blocks = pl.ds(2 * g, 2)
@@ -242,12 +243,10 @@
 
     lefts[0].wait()
     compute(0)
-    first(0)
 
     lefts[1].wait()
     halos[5].wait_recv()
     compute(1)
-    first(1)
 
     @pl.when(has_distant)
     def _():
@@ -257,7 +256,6 @@
 
     lefts[2].wait()
     compute(2)
-    first(2)
     pass_on(0)
 
     @pl.when(has_distant)
@@ -268,7 +266,6 @@
 
     lefts[3].wait()
     compute(3)
-    first(3)
     second(0)
     pass_on(1)
     second(1)

time: 34.9 us -> 34.7 us (level)
  no operation moved by 1% of the time
where the time goes in v5:
time: 34.7 us; the launch traced here: 34.5 us
  Pallas kernels  32.9 us (95%)
  local copies, waits for them, and re-layouts  1.57 us (5%)
    pallas_call x1, Pallas kernels, on_device(): pl.pallas_call(functools.partial(kernel, lax.axis_size('sec')), out_shape...  32.9 us
    unnamed x1, local copies, waits for them, and re-layouts  1.57 us

profile of v5, /device:TPU:384, one launch (start us, length us, event | category | flops | bytes accessed | tf_op | source)
XLA Modules:
  0.0 34.5 jit_solution(1210191112986679035)
XLA Ops:
  0.0 32.9 %shard_map.64 = bf16[4,4,16,256]{3,2,1,0:T(8,128)(2,1)} custom-call(bf16[4,4,256,256]{3,2,1,0:T(8,128)(2,1)} %psi.1, bf16[4,4,256,256]{3,2,1,0:T(8,128)(2,1)} %left.1, bf16[4,256,256]{2,1,0:T(8,128)(2,1)} %right.1, f32[4,4,4]{2,1,0:T(4,128)} %ops.1, s32[4,4]{1,0:T(4,128)} %coupling.1, s32[4]{0:T(128)} %live.1), custom_call_target="tpu_custom_call" | custom-call | tf_op jit(solution)/shard_map/pallas_call | solution.py:292
  32.9 1.6 %copy.8 = bf16[4,4,16,256]{3,2,1,0:T(8,128)(2,1)} copy(bf16[4,4,16,256]{3,2,1,0:T(8,128)(2,1)} %shard_map.64) | data formatting | bytes 262144
